TPU v7x, 256 devices: a whole 4x4x8 slice. The times are simulated.
256 devices in a mesh: blk: 16 (over x_hi, z), wide: 16 (over y, x_lo, core).
Axes of the slice: x: 4 (x_hi: 2, x_lo: 2; x = x_hi * 2 + x_lo), y: 4, z: 8, core: 2. Of those that a mesh axis runs over, the one named last changes fastest.
Arguments:
- blocks: bfloat16 [4096, 64, 4096], P(('blk', 'wide')), may hold values from -24 to 24
- block_row: int32 [4096], P(('blk', 'wide')), may hold values from 0 to 3
- block_depth: int32 [4096], P(('blk', 'wide')), may hold values from 0 to 15
- live: int32 [4096], P(('blk', 'wide')), may hold values from 0 to 1, as said below
- factor_b: bfloat16 [1024, 256], P('blk'), may hold values from -6 to 6
- factor_c: bfloat16 [1024, 256], replicated, may hold values from -6 to 6
Outputs:
- factor_a: bfloat16 [4096, 256], P('wide')
- factor_b_new: bfloat16 [1024, 256], P(('blk', 'wide'))
Inputs may be any that keep to these rules, and one draw needn't show every extreme that they name: 1 marks a slot that holds a block, 0 an empty one; the share of live slots differs between devices, and slots 0 to 15 are all live.
All inputs are finite; a program needn't handle non-finite values.
Results may differ from a plain program's by a relative error of at most 0.0091.
Values may be sent and summed in bfloat16 or wider, within the bound.
A program may use at most 64 MiB of HBM per device.

v0:
```python
import jax
import jax.numpy as jnp
from jax import lax
from jax.sharding import PartitionSpec as P

BLOCK = 64
ROW_BLOCKS = 4
ROWS_C = 1024
RIDGE = 0.05


def factor_solve(partial_rows, gram):
    size = gram.shape[0]
    system = gram + RIDGE * jnp.eye(size, dtype=jnp.float32)
    lower = jnp.linalg.cholesky(system)
    solved = jax.scipy.linalg.cho_solve((lower, True), partial_rows.T)
    return solved.T * (0.125 / BLOCK)


def first_term(block, brows, crows):
    width = brows.shape[1]
    paired = (brows.astype(jnp.float32)[:, None, :] * crows.astype(jnp.float32)[None, :, :]).astype(
        jnp.bfloat16
    )
    return jnp.dot(block, paired.reshape(-1, width), preferred_element_type=jnp.float32)


def second_term(block, arows, crows):
    edge = arows.shape[0]
    paired = (arows.astype(jnp.float32)[:, None, :] * crows.astype(jnp.float32)[None, :, :]).astype(
        jnp.bfloat16
    )
    cube = block.reshape(edge, edge, edge)
    return lax.dot_general(
        cube, paired, (((0, 2), (0, 1)), ((), ())), preferred_element_type=jnp.float32
    )


def per_device(blocks, block_row, block_depth, live, factor_b, factor_c):
    edge = blocks.shape[1]
    slot_total = blocks.shape[0]
    rank = factor_c.shape[1]
    slice_rows = ROW_BLOCKS * BLOCK
    weights = live.astype(jnp.float32)
    gram_c = jnp.dot(factor_c.T, factor_c, preferred_element_type=jnp.float32) / ROWS_C
    empty_rows = jnp.zeros((slice_rows, rank), jnp.float32)
    gram_scale = lax.axis_size("blk") * edge
    piece = lax.all_gather(factor_b, "blk", axis=0, tiled=True)
    count = piece.shape[0] // edge

    def one_slot(step, acc):
        brows = lax.dynamic_slice_in_dim(piece, step * edge, edge, 0)
        crows = lax.dynamic_slice_in_dim(factor_c, block_depth[step] * edge, edge, 0)
        term = first_term(blocks[step], brows, crows) * weights[step]
        row = block_row[step] * edge
        current = lax.dynamic_slice_in_dim(acc, row, edge, 0)
        return lax.dynamic_update_slice_in_dim(acc, current + term, row, 0)

    mttkrp_part = lax.fori_loop(0, count, one_slot, empty_rows)
    panel_gram = jnp.dot(factor_b.T, factor_b, preferred_element_type=jnp.float32)
    gram_b = lax.psum(panel_gram, "blk") / gram_scale
    system_a = gram_c * gram_b
    total_rows = lax.axis_size("wide") * slice_rows
    mttkrp_a = lax.psum(mttkrp_part, "blk")
    factor_a = factor_solve(mttkrp_a, system_a).astype(jnp.bfloat16)
    slice_gram = jnp.dot(factor_a.T, factor_a, preferred_element_type=jnp.float32)
    gram_a = lax.psum(slice_gram, "wide") / total_rows

    def second_part(slot):
        arows = lax.dynamic_slice_in_dim(factor_a, block_row[slot] * edge, edge, 0)
        crows = lax.dynamic_slice_in_dim(factor_c, block_depth[slot] * edge, edge, 0)
        return second_term(blocks[slot], arows, crows) * weights[slot]

    partials = lax.map(second_part, jnp.arange(slot_total, dtype=jnp.int32))
    flat = partials.reshape(slot_total * edge, rank)
    mttkrp_b = lax.psum_scatter(flat, ("blk", "wide"), scatter_dimension=0, tiled=True)
    factor_b_new = factor_solve(mttkrp_b, gram_c * gram_a).astype(jnp.bfloat16)
    return (factor_a, factor_b_new)


def solution(mesh):
    in_specs = (
        P(("blk", "wide"), None, None),
        P(("blk", "wide")),
        P(("blk", "wide")),
        P(("blk", "wide")),
        P("blk", None),
        P(),
    )
    out_specs = (P("wide", None), P(("blk", "wide"), None))
    return jax.shard_map(
        per_device, mesh=mesh, in_specs=in_specs, out_specs=out_specs, check_vma=False
    )
```

profile of v0, /device:TPU:2, one launch (start us, length us, event | category | flops | bytes accessed | tf_op | source)
XLA Modules:
  0.0 851.8 jit_solution(16122719357660556276)
XLA Ops:
  7.2 46.3 %all_gather.3 = bf16[1024,256]{1,0:T(8,128)(2,1)S(1)} all-gather(bf16[64,256]{1,0:T(8,128)(2,1)} %param.15), channel_id=1, replica_groups=mesh['blk'=16,'wide'=16] {'blk'}, dimensions={0}, use_global_device_ids=true | all-gather | bytes 557056 | tf_op jit(solution)/shard_map/all_gather | solution.py:48
  56.0 134.5 %while.25 = (s32[]{:T(128)}, f32[256,256]{1,0:T(8,128)S(1)}, s32[16]{0:T(128)}, bf16[16,64,4096]{2,1,0:T(8,128)(2,1)}, bf16[1024,256]{1,0:T(8,128)(2,1)S(1)}, /*...) while((s32[]{:T(128)}, f32[256,256]{1,0:T(8,128)S(1)}, ...), condition=%wide.region_6.8_spmd, body=%wide.region_5.7_spmd.sunk | while | flops 136380432 | bytes 5178687 | solution.py:59
  62.2 2.2 fusion.74
  70.6 2.2 fusion.74
  79.0 2.2 fusion.74
  87.4 2.2 fusion.74
  95.8 2.2 fusion.74
  104.2 2.2 fusion.74
  112.6 2.2 fusion.74
  121.0 2.2 fusion.74
  129.5 2.2 fusion.74
  137.9 2.2 fusion.74
  146.3 2.2 fusion.74
  154.7 2.2 fusion.74
  163.1 2.2 fusion.74
  171.5 2.2 fusion.74
  179.9 2.2 fusion.74
  188.3 2.2 fusion.74
  191.3 152.3 %all-reduce.11.cloned.1.call-done = (f32[256,256]{0,1:T(8,128)}, f32[256,256]{0,1:T(8,128)}) async-done(((f32[256,256]{0,1:T(8,128)}, f32[256,256]{0,1:T(8,128)}), (f32[256,256]{0,1:T(8,128)}, f32[256,256]{0,1:T(8,128)})) %all-reduce.11.cloned.1.call-update) | async-done | bytes 524304 | tf_op jit(solution)/shard_map/psum | solution.py:64
  345.6 11.7 %cholesky.130 = f32[128,128]{1,0:T(8,128)S(1)} custom-call(f32[128,128]{1,0:T(8,128)S(1)} %cholesky.194), custom_call_target="Cholesky" | custom-call | tf_op jit(solution)/shard_map/jit(cholesky)/cholesky | solution.py:15
  357.4 9.8 %custom-call.25 = f32[1,128,128]{1,2,0:T(8,128)S(1)} custom-call(f32[1,128,128]{2,1,0:T(8,128)S(1)} %get-tuple-element.324), custom_call_target="InvertDiagBlocksLowerTriangular" | custom-call | tf_op jit(solution)/shard_map/jit(cholesky)/cholesky | solution.py:15
  367.7 11.7 %cholesky.147 = f32[128,128]{1,0:T(8,128)S(1)} custom-call(f32[128,128]{1,0:T(8,128)S(1)} %convolution_subtract_fusion.3), custom_call_target="Cholesky" | custom-call | tf_op jit(solution)/shard_map/jit(cholesky)/cholesky | solution.py:15
  381.9 4.4 while.27
  386.3 19.7 %custom-call.22 = f32[2,128,128]{1,2,0:T(8,128)S(1)} custom-call(f32[2,128,128]{2,1,0:T(8,128)S(1)} %get-tuple-element.198), custom_call_target="InvertDiagBlocksLowerTriangular" | custom-call | tf_op jit(solution)/shard_map/jit(_cho_solve)/triangular_solve | solution.py:16
  409.0 176.0 %while.26 = (s32[]{:T(128)}, f32[16,64,256]{2,1,0:T(8,128)}, s32[16]{0:T(128)S(1)}, bf16[16,64,4096]{2,1,0:T(8,128)(2,1)}, s32[16]{0:T(128)S(1)}, /*index=5*/bf1...) while((s32[]{:T(128)}, f32[16,64,256]{2,1,0:T(8,128)}, ...), condition=%wide.region_10.12_spmd, body=%wide.region_9.11_spmd.sunk | while | flops 136364048 | bytes 3016007 | solution.py:74
  583.0 1.9 fusion.76
  586.2 11.7 %cholesky.164 = f32[128,128]{1,0:T(8,128)S(1)} custom-call(f32[128,128]{1,0:T(8,128)S(1)} %cholesky.197), custom_call_target="Cholesky" | custom-call | tf_op jit(solution)/shard_map/jit(cholesky)/cholesky | solution.py:15
  597.9 9.8 %custom-call.26 = f32[1,128,128]{1,2,0:T(8,128)S(1)} custom-call(f32[1,128,128]{2,1,0:T(8,128)S(1)} %get-tuple-element.322), custom_call_target="InvertDiagBlocksLowerTriangular" | custom-call | tf_op jit(solution)/shard_map/jit(cholesky)/cholesky | solution.py:15
  608.2 11.7 %cholesky.181 = f32[128,128]{1,0:T(8,128)S(1)} custom-call(f32[128,128]{1,0:T(8,128)S(1)} %convolution_subtract_fusion.2), custom_call_target="Cholesky" | custom-call | tf_op jit(solution)/shard_map/jit(cholesky)/cholesky | solution.py:15
  622.9 4.3 while.28
  627.3 19.7 %custom-call.23 = f32[2,128,128]{1,2,0:T(8,128)S(1)} custom-call(f32[2,128,128]{2,1,0:T(8,128)S(1)} %get-tuple-element.206), custom_call_target="InvertDiagBlocksLowerTriangular" | custom-call | tf_op jit(solution)/shard_map/jit(_cho_solve)/triangular_solve | solution.py:16
  646.9 195.7 %all-reduce.9.cloned.1.call-done = f32[1024,256]{1,0:T(8,128)} async-done(((f32[1024,256]{1,0:T(8,128)}), f32[1024,256]{1,0:T(8,128)}) %all-reduce.9.cloned.1.call-update) | async-done | bytes 1048592
  (303 shorter events, 218.5 us)
Async XLA Ops:
  7.2 336.4 %all-reduce.11.cloned.1.call-start = ((), (), s32[]{:S(2)}) async-start(), calls=%async_computation.2 | async-start | bytes 1048576 | tf_op jit(solution)/shard_map/psum | solution.py:64
  190.5 0.7 copy-start
  191.3 393.7 %all-reduce.7.cloned.1.call-start = ((), (), s32[]{:S(2)}) async-start(), calls=%async_computation | async-start | bytes 524288 | tf_op jit(solution)/shard_map/psum | solution.py:67
  343.6 62.3 %copy-start.2 = (f32[256,256]{0,1:T(8,128)S(1)}, f32[256,256]{0,1:T(8,128)}, u32[]{:S(2)}) copy-start(f32[256,256]{0,1:T(8,128)} %get-tuple-element.311) | copy-start | bytes 786436
  345.6 63.3 %copy-start.3 = (s32[16]{0:T(128)S(1)}, s32[16]{0:T(128)}, u32[]{:S(2)}) copy-start(s32[16]{0:T(128)} %get-tuple-element.639) | copy-start | bytes 196
  345.6 63.3 %copy-start.4 = (s32[16]{0:T(128)S(1)}, s32[16]{0:T(128)}, u32[]{:S(2)}) copy-start(s32[16]{0:T(128)} %get-tuple-element.640) | copy-start | bytes 196
  408.8 433.9 %all-reduce.9.cloned.1.call-start = ((), (), s32[]{:S(2)}) async-start(), calls=%async_computation.1 | async-start | bytes 2097152
  584.9 260.4 %copy-start.1 = (bf16[256,256]{1,0:T(8,128)(2,1)}, bf16[256,256]{1,0:T(8,128)(2,1)S(1)}, u32[]{:S(2)}) copy-start(bf16[256,256]{1,0:T(8,128)(2,1)S(1)} %get-tuple-element.633) | copy-start | bytes 393220
Sparse Core Ops, SparseCore 0:
  191.4 152.1 all-reduce.10
  408.9 118.2 all-reduce.6
  585.1 257.5 all-reduce.8
where the time goes:
time: 858 us; the launch traced here: 852 us
  waiting for transfers between devices  348 us (41%)
  other arithmetic  146 us (17%)
  local copies, waits for them, and re-layouts  142 us (17%)
  loops' own time  79.6 us (9%)
  matrix products  73.4 us (9%)
  blocking collectives  46.3 us (5%)
  between operations  16.6 us (2%)
    unnamed x4, waiting for transfers between devices  196 us
    psum x1, waiting for transfers between devices, per_device(): mttkrp_a = lax.psum(mttkrp_part, 'blk')  152 us
    another operation x13, other arithmetic, factor_solve(): lower = jnp.linalg.cholesky(system)  68.6 us
    another operation x1, loops' own time, per_device(): partials = lax.map(second_part, jnp.arange(slot_total, dtype=jnp.int32))  55.9 us
    all_gather x1, blocking collectives, per_device(): piece = lax.all_gather(factor_b, 'blk', axis=0, tiled=True)  46.3 us
    another operation x5, other arithmetic, factor_solve(): solved = jax.scipy.linalg.cho_solve((lower, True), partial_rows.T)  39.4 us
    dot_general x16, matrix products, first_term(): jnp.dot(block, paired.reshape(-1, width), preferred_element_type=jnp.floa...  35.1 us
    dot_general x16, matrix products, second_term(): lax.dot_general(cube, paired, (((0, 2), (0, 1)), ((), ())), preferred_ele...  29.8 us
  transfers between devices with their start and end apart: 3, of which 2 were waited for; matrix products, arithmetic and copies ran while one was open for 21% of the time, Pallas kernels for 0%

commit v1 on v0

--- a/solution.py
+++ b/solution.py
@@ -61,7 +61,7 @@
     gram_b = lax.psum(panel_gram, "blk") / gram_scale
     system_a = gram_c * gram_b
     total_rows = lax.axis_size("wide") * slice_rows
-    mttkrp_a = lax.psum(mttkrp_part, "blk")
+    mttkrp_a = jax.lax.all_gather(mttkrp_part, "blk").sum(axis=0)
     factor_a = factor_solve(mttkrp_a, system_a).astype(jnp.bfloat16)
     slice_gram = jnp.dot(factor_a.T, factor_a, preferred_element_type=jnp.float32)
     gram_a = lax.psum(slice_gram, "wide") / total_rows

time: 858 us -> 740 us (0.86)
  waiting for transfers between devices: 348 us -> 228 us
    psum x1, waiting for transfers between devices: 152 us -> 0.02 us  [per_device(): gram_b = lax.psum(panel_gram, 'blk') / gram_scale]
    all_gather x0 -> x1, waiting for transfers between devices: none -> 32.5 us  [per_device(): mttkrp_a = jax.lax.all_gather(mttkrp_part, 'blk').sum(axis=0)]
    unnamed x4 -> x5, waiting for transfers between devices: 196 us -> 195 us
  transfers between devices with their start and end apart: 3 -> 4, of which waited for: 2 -> 2; matrix products, arithmetic and copies ran while one was open for 21% -> 48% of each run, Pallas kernels for 0% -> 0%
where the time goes in v1:
time: 740 us; the launch traced here: 734 us
  waiting for transfers between devices  228 us (31%)
  other arithmetic  149 us (20%)
  local copies, waits for them, and re-layouts  142 us (19%)
  loops' own time  79.5 us (11%)
  matrix products  73.3 us (10%)
  blocking collectives  46.4 us (6%)
  between operations  16.7 us (2%)
    unnamed x5, waiting for transfers between devices  195 us
    another operation x13, other arithmetic, factor_solve(): lower = jnp.linalg.cholesky(system)  68.7 us
    another operation x1, loops' own time, per_device(): partials = lax.map(second_part, jnp.arange(slot_total, dtype=jnp.int32))  55.8 us
    all_gather x1, blocking collectives, per_device(): piece = lax.all_gather(factor_b, 'blk', axis=0, tiled=True)  46.4 us
    another operation x5, other arithmetic, factor_solve(): solved = jax.scipy.linalg.cho_solve((lower, True), partial_rows.T)  39.4 us
    dot_general x16, matrix products, first_term(): jnp.dot(block, paired.reshape(-1, width), preferred_element_type=jnp.floa...  35.2 us
    all_gather x1, waiting for transfers between devices, per_device(): mttkrp_a = jax.lax.all_gather(mttkrp_part, 'blk').sum(axis=0)  32.5 us
    dot_general x16, matrix products, second_term(): lax.dot_general(cube, paired, (((0, 2), (0, 1)), ((), ())), preferred_ele...  29.7 us
  transfers between devices with their start and end apart: 4, of which 2 were waited for; matrix products, arithmetic and copies ran while one was open for 48% of the time, Pallas kernels for 0%

profile of v1, /device:TPU:2, one launch (start us, length us, event | category | flops | bytes accessed | tf_op | source)
XLA Modules:
  0.0 734.0 jit_solution(8826509394797026242)
XLA Ops:
  9.1 46.4 %all_gather.9 = bf16[1024,256]{1,0:T(8,128)(2,1)S(1)} all-gather(bf16[64,256]{1,0:T(8,128)(2,1)} %param.15), channel_id=1, replica_groups=mesh['blk'=16,'wide'=16] {'blk'}, dimensions={0}, use_global_device_ids=true | all-gather | bytes 557056 | tf_op jit(solution)/shard_map/all_gather | solution.py:48
  56.1 134.6 %while.25 = (s32[]{:T(128)}, f32[256,256]{1,0:T(8,128)S(1)}, s32[16]{0:T(128)}, bf16[16,64,4096]{2,1,0:T(8,128)(2,1)}, bf16[1024,256]{1,0:T(8,128)(2,1)S(1)}, /*...) while((s32[]{:T(128)}, f32[256,256]{1,0:T(8,128)S(1)}, ...), condition=%wide.region_6.8_spmd, body=%wide.region_5.7_spmd.sunk | while | flops 136380432 | bytes 5178187 | solution.py:59
  62.3 2.2 fusion.74
  70.8 2.2 fusion.74
  79.2 2.2 fusion.74
  87.6 2.2 fusion.74
  96.0 2.2 fusion.74
  104.4 2.2 fusion.74
  112.8 2.2 fusion.74
  121.2 2.2 fusion.74
  129.7 2.2 fusion.74
  138.1 2.2 fusion.74
  146.5 2.2 fusion.74
  154.9 2.2 fusion.74
  163.3 2.2 fusion.74
  171.7 2.2 fusion.74
  180.1 2.2 fusion.74
  188.5 2.2 fusion.74
  193.5 11.7 %cholesky.130 = f32[128,128]{1,0:T(8,128)S(1)} custom-call(f32[128,128]{1,0:T(8,128)S(1)} %cholesky.194), custom_call_target="Cholesky" | custom-call | tf_op jit(solution)/shard_map/jit(cholesky)/cholesky | solution.py:15
  205.3 9.8 %custom-call.25 = f32[1,128,128]{1,2,0:T(8,128)S(1)} custom-call(f32[1,128,128]{2,1,0:T(8,128)S(1)} %get-tuple-element.322), custom_call_target="InvertDiagBlocksLowerTriangular" | custom-call | tf_op jit(solution)/shard_map/jit(cholesky)/cholesky | solution.py:15
  215.7 11.7 %cholesky.147 = f32[128,128]{1,0:T(8,128)S(1)} custom-call(f32[128,128]{1,0:T(8,128)S(1)} %convolution_subtract_fusion.3), custom_call_target="Cholesky" | custom-call | tf_op jit(solution)/shard_map/jit(cholesky)/cholesky | solution.py:15
  229.7 4.3 while.27
  234.0 19.7 %custom-call.22 = f32[2,128,128]{1,2,0:T(8,128)S(1)} custom-call(f32[2,128,128]{2,1,0:T(8,128)S(1)} %get-tuple-element.198), custom_call_target="InvertDiagBlocksLowerTriangular" | custom-call | tf_op jit(solution)/shard_map/jit(_cho_solve)/triangular_solve | solution.py:16
  253.7 32.5 %all-gather.3.cloned.1.call-done = f32[4096,256]{1,0:T(8,128)} async-done(((f32[256,256]{1,0:T(8,128)}), f32[4096,256]{1,0:T(8,128)}) %all-gather.3.cloned.1.call-update) | async-done | bytes 4194320 | tf_op jit(solution)/shard_map/all_gather | solution.py:64
  286.2 2.5 reduce_sum.9
  291.7 176.0 %while.26 = (s32[]{:T(128)}, f32[16,64,256]{2,1,0:T(8,128)}, s32[16]{0:T(128)S(1)}, bf16[16,64,4096]{2,1,0:T(8,128)(2,1)}, s32[16]{0:T(128)S(1)}, /*index=5*/bf1...) while((s32[]{:T(128)}, f32[16,64,256]{2,1,0:T(8,128)}, ...), condition=%wide.region_10.12_spmd, body=%wide.region_9.11_spmd.sunk | while | flops 136364048 | bytes 3015507 | solution.py:74
  468.9 11.7 %cholesky.164 = f32[128,128]{1,0:T(8,128)S(1)} custom-call(f32[128,128]{1,0:T(8,128)S(1)} %cholesky.197), custom_call_target="Cholesky" | custom-call | tf_op jit(solution)/shard_map/jit(cholesky)/cholesky | solution.py:15
  480.8 9.8 %custom-call.26 = f32[1,128,128]{1,2,0:T(8,128)S(1)} custom-call(f32[1,128,128]{2,1,0:T(8,128)S(1)} %get-tuple-element.320), custom_call_target="InvertDiagBlocksLowerTriangular" | custom-call | tf_op jit(solution)/shard_map/jit(cholesky)/cholesky | solution.py:15
  491.2 11.7 %cholesky.181 = f32[128,128]{1,0:T(8,128)S(1)} custom-call(f32[128,128]{1,0:T(8,128)S(1)} %convolution_subtract_fusion.2), custom_call_target="Cholesky" | custom-call | tf_op jit(solution)/shard_map/jit(cholesky)/cholesky | solution.py:15
  505.7 4.5 while.28
  510.3 19.7 %custom-call.23 = f32[2,128,128]{1,2,0:T(8,128)S(1)} custom-call(f32[2,128,128]{2,1,0:T(8,128)S(1)} %get-tuple-element.206), custom_call_target="InvertDiagBlocksLowerTriangular" | custom-call | tf_op jit(solution)/shard_map/jit(_cho_solve)/triangular_solve | solution.py:16
  530.0 194.9 %all-reduce.10.cloned.1.call-done = f32[1024,256]{1,0:T(8,128)} async-done(((f32[1024,256]{1,0:T(8,128)}), f32[1024,256]{1,0:T(8,128)}) %all-reduce.10.cloned.1.call-update) | async-done | bytes 1048592
  (305 shorter events, 220.6 us)
Async XLA Ops:
  7.2 184.4 %all-reduce.6.cloned.1.call-start = ((), (), s32[]{:S(2)}) async-start(), calls=%async_computation | async-start | bytes 524288 | tf_op jit(solution)/shard_map/psum | solution.py:61
  9.0 277.2 %all-gather.3.cloned.1.call-start = ((), (), s32[]{:S(2)}) async-start(), calls=%async_computation.2 | async-start | bytes 4456448 | tf_op jit(solution)/shard_map/all_gather | solution.py:64
  190.8 0.7 copy-start
  191.5 276.2 %all-reduce.8.cloned.1.call-start = ((), (), s32[]{:S(2)}) async-start(), calls=%async_computation.1 | async-start | bytes 524288 | tf_op jit(solution)/shard_map/psum | solution.py:67
  233.9 57.7 %copy-start.2 = (s32[16]{0:T(128)S(1)}, s32[16]{0:T(128)}, u32[]{:S(2)}) copy-start(s32[16]{0:T(128)} %get-tuple-element.635) | copy-start | bytes 196
  234.0 57.7 %copy-start.3 = (s32[16]{0:T(128)S(1)}, s32[16]{0:T(128)}, u32[]{:S(2)}) copy-start(s32[16]{0:T(128)} %get-tuple-element.636) | copy-start | bytes 196
  291.6 433.2 %all-reduce.10.cloned.1.call-start = ((), (), s32[]{:S(2)}) async-start(), calls=%async_computation.3 | async-start | bytes 2097152
  467.7 259.8 %copy-start.1 = (bf16[256,256]{1,0:T(8,128)(2,1)}, bf16[256,256]{1,0:T(8,128)(2,1)S(1)}, u32[]{:S(2)}) copy-start(bf16[256,256]{1,0:T(8,128)(2,1)S(1)} %get-tuple-element.631) | copy-start | bytes 393220
Sparse Core Ops, SparseCore 0:
  10.6 159.0 all-reduce.5
  191.6 94.5 all-gather.2
  291.7 117.6 all-reduce.7
  467.8 256.9 all-reduce.9
